TPU v7x, 128 devices: a whole 4x4x4 slice. The times are simulated.
128 devices in a mesh: row: 8 (over x, z_hi), col: 16 (over z_lo, y, core).
Axes of the slice: x: 4, y: 4, z: 4 (z_hi: 2, z_lo: 2; z = z_hi * 2 + z_lo), core: 2. Of those that a mesh axis runs over, the one named last changes fastest.
Arguments:
- window: float32 [12288, 12288], P('row', 'col'), may hold values from -6 to 6
- reflectors: float32 [2, 12288, 256], P(None, 'row', 'col'), may hold values from -0.0546875 to 0.0546875
- factors: float32 [2, 256, 256], replicated, may hold values from -0.375 to 0.375
Outputs:
- updated: float32 [12288, 12288], P('row', 'col')
All inputs are finite; a program needn't handle non-finite values.
Results may differ from a plain program's by a relative error of at most 0.0001.
Values sent between devices are 32-bit elements; how exact they have to be, the bound alone decides.
A program may use at most 128 MiB of HBM per device.

v0:
```python
import jax
import jax.numpy as jnp
from jax import lax
from jax.sharding import PartitionSpec as P

highest = lax.Precision.HIGHEST


def product(factor_one, factor_two):
    return jnp.dot(factor_one, factor_two, precision=highest, preferred_element_type=jnp.float32)


def body(window, reflectors, factors):
    row_index = lax.axis_index("row")
    col_index = lax.axis_index("col")
    row_count = lax.axis_size("row")
    col_count = lax.axis_size("col")
    rows_loc = window.shape[0]
    cols_loc = window.shape[1]
    updated = window
    for panel in range(reflectors.shape[0]):
        sliver = reflectors[panel]
        factor = factors[panel]
        everything = lax.all_gather(sliver[None], ("row", "col"), axis=0, tiled=True)
        piece_cols = sliver.shape[1]
        vectors = everything.reshape(row_count, col_count, rows_loc, piece_cols)
        vectors = vectors.transpose(0, 2, 1, 3).reshape(
            row_count * rows_loc, col_count * piece_cols
        )
        local_vectors = lax.dynamic_slice_in_dim(vectors, row_index * rows_loc, rows_loc, 0)
        column_vectors = lax.dynamic_slice_in_dim(vectors, col_index * cols_loc, cols_loc, 0)
        partial_value = product(local_vectors.T, updated)
        projected = lax.psum(partial_value, "row")
        updated = updated - product(local_vectors, product(factor.T, projected))
        image_sum = lax.psum(product(updated, column_vectors), "col")
        updated = updated - product(product(image_sum, factor), column_vectors.T)
    return updated


def solution(mesh):
    placed = (P("row", "col"), P(None, "row", "col"), P())
    return jax.shard_map(
        body, mesh=mesh, in_specs=placed, out_specs=P("row", "col"), check_vma=False
    )
```

profile of v0, /device:TPU:1, one launch (start us, length us, event | category | flops | bytes accessed | tf_op | source)
XLA Modules:
  0.0 693.6 jit_solution(10006630515930654587)
XLA Ops:
  6.5 1.6 fusion.32
  8.2 0.0 all-reduce.5.cloned.1.call-start
  8.2 78.9 %all-gather.3.cloned.1.call-done = f32[128,1536,16]{1,2,0:T(8,128)} async-done(((f32[1,1536,16]{1,2,0:T(8,128)}), f32[128,1536,16]{1,2,0:T(8,128)}) %all-gather.3.cloned.1.call-update) | async-done | bytes 12582928 | tf_op jit(solution)/shard_map/all_gather | solution.py:24
  87.1 19.4 %copy.6 = f32[8,16,1536,16]{2,0,3,1:T(8,128)} copy(f32[8,16,1536,16]{2,3,1,0:T(8,128)} %bitcast.49) | data formatting | bytes 25165824 | tf_op jit(solution)/shard_map/reshape | solution.py:26
  106.6 20.8 %copy.8 = f32[32,8,8,1536]{3,1,2,0:T(8,128)} copy(f32[32,8,8,1536]{3,2,1,0:T(8,128)} %bitcast.36) | data formatting | bytes 25165824
  127.3 16.7 %fusion.4 = f32[256,768]{1,0:T(8,128)} fusion(f32[1536,768]{1,0:T(8,128)S(1)} %bitcast.47, f32[12288,256]{0,1:T(8,128)} %bitcast.38, s32[]{:T(128)S(6)} %select_n.8), kind=kOutput, calls=%fused_computation.8 | convolution fusion | flops 3623878656 | bytes 7077892 | tf_op jit(solution)/shard_map/dot_general | solution.py:10
  144.1 0.0 all-gather.5.cloned.1.call-start
  144.1 0.7 all-gather.5.cloned.1.call-update
  144.8 0.0 all-reduce.7.cloned.1.call-start
  144.9 80.3 %all-reduce.5.cloned.1.call-done = f32[256,768]{1,0:T(8,128)} async-done(((f32[256,768]{1,0:T(8,128)}), f32[256,768]{1,0:T(8,128)}) %all-reduce.5.cloned.1.call-update) | async-done | bytes 786448 | tf_op jit(solution)/shard_map/psum | solution.py:33
  225.2 2.5 fusion.18
  227.7 10.9 %convolution_subtract_fusion.3 = f32[1536,768]{1,0:T(8,128)S(1)} fusion(f32[1536,768]{1,0:T(8,128)} %param.3, f32[768,256]{1,0:T(8,128)S(1)} %fusion.18, f32[12288,256]{0,1:T(8,128)} %bitcast.39, s32[]{:T(128)S(6)} %select_n.8), kind=kOutput, calls=%fused_computation.3 | convolution fusion | flops 3625058304 | bytes 11796484 | tf_op jit(solution)/shard_map/dot_general | solution.py:10
  238.6 2.2 copy-done
  240.8 6.6 fusion.10
  247.4 0.0 all-reduce.9.cloned.1.call-start
  247.5 57.3 %all-gather.5.cloned.1.call-done = f32[128,1536,16]{1,2,0:T(8,128)} async-done(((f32[1,1536,16]{1,2,0:T(8,128)}), f32[128,1536,16]{1,2,0:T(8,128)}) %all-gather.5.cloned.1.call-update) | async-done | bytes 12582928 | tf_op jit(solution)/shard_map/all_gather | solution.py:24
  304.8 19.4 %copy.7 = f32[8,16,1536,16]{2,0,3,1:T(8,128)} copy(f32[8,16,1536,16]{2,3,1,0:T(8,128)} %bitcast.48) | data formatting | bytes 25165824 | tf_op jit(solution)/shard_map/reshape | solution.py:26
  324.2 20.6 %copy.9 = f32[32,8,8,1536]{3,1,2,0:T(8,128)} copy(f32[32,8,8,1536]{3,2,1,0:T(8,128)} %bitcast.37) | data formatting | bytes 25165824
  344.7 83.1 %all-reduce.7.cloned.1.call-done = f32[1536,256]{1,0:T(8,128)} async-done(((f32[1536,256]{1,0:T(8,128)}), f32[1536,256]{1,0:T(8,128)}) %all-reduce.7.cloned.1.call-update) | async-done | bytes 1572880 | tf_op jit(solution)/shard_map/psum | solution.py:35
  427.8 2.8 fusion.16
  430.6 6.4 convolution_subtract_fusion.2
  437.1 2.2 copy-done.1
  439.2 6.6 fusion.1
  445.8 0.3 all-reduce.11.cloned.1.call-start
  446.1 83.0 %all-reduce.9.cloned.1.call-done = f32[256,768]{1,0:T(8,128)} async-done(((f32[256,768]{1,0:T(8,128)}), f32[256,768]{1,0:T(8,128)}) %all-reduce.9.cloned.1.call-update) | async-done | bytes 786448 | tf_op jit(solution)/shard_map/psum | solution.py:33
  529.1 2.5 fusion.14
  531.6 10.9 %convolution_subtract_fusion.1 = f32[1536,768]{1,0:T(8,128)S(1)} fusion(f32[1536,768]{1,0:T(8,128)} %copy-done.1, f32[768,256]{1,0:T(8,128)S(1)} %fusion.14, f32[12288,256]{0,1:T(8,128)} %bitcast.43, s32[]{:T(128)S(6)} %select_n.8), kind=kOutput, calls=%fused_computation.1 | convolution fusion | flops 3625058304 | bytes 11796484 | tf_op jit(solution)/shard_map/dot_general | solution.py:10
  542.5 2.2 copy-done.2
  544.7 6.5 fusion.7
  551.2 124.8 %all-reduce.11.cloned.1.call-done = f32[1536,256]{1,0:T(8,128)} async-done(((f32[1536,256]{1,0:T(8,128)}), f32[1536,256]{1,0:T(8,128)}) %all-reduce.11.cloned.1.call-update) | async-done | bytes 1572880 | tf_op jit(solution)/shard_map/psum | solution.py:35
  676.0 2.8 fusion.12
  678.8 7.5 %convolution_subtract_fusion = f32[1536,768]{1,0:T(8,128)} fusion(f32[1536,768]{1,0:T(8,128)} %copy-done.2, f32[1536,256]{1,0:T(8,128)S(1)} %fusion.12, f32[12288,256]{0,1:T(8,128)} %bitcast.45, s32[]{:T(128)S(6)} %select_n.9), kind=kOutput, calls=%fused_computation | convolution fusion | flops 3625058304 | bytes 11796484 | tf_op jit(solution)/shard_map/dot_general | solution.py:10
  (16 shorter events, 0.1 us)
Async XLA Ops:
  6.5 80.6 %all-gather.3.cloned.1.call-start = ((), (), s32[]{:S(2)}) async-start(), calls=%async_computation | async-start | bytes 12681216 | tf_op jit(solution)/shard_map/all_gather | solution.py:24
  8.2 217.0 %all-reduce.5.cloned.1.call-start = ((), (), s32[]{:S(2)}) async-start(), calls=%async_computation.1 | async-start | bytes 1572864 | tf_op jit(solution)/shard_map/psum | solution.py:33
  87.1 40.2 %slice-start = ((s8[4718592]{0:T(1024)(128)(4,1)}), s8[4194304]{0:T(1024)(128)(4,1)S(1)}, s32[]{:S(2)}) async-start(s8[4718592]{0:T(1024)(128)(4,1)} %bitcast.46), calls=%async_computation.6 | async-start | bytes 8388608
  106.6 20.8 %slice-start.1 = ((s8[4718592]{0:T(1024)(128)(4,1)}), s8[524288]{0:T(1024)(128)(4,1)S(1)}, s32[]{:S(2)}) async-start(s8[4718592]{0:T(1024)(128)(4,1)} %bitcast.46), calls=%async_computation.7 | async-start | bytes 1048576
  127.3 97.8 %copy-start.3 = (f32[2,256,256]{2,1,0:T(8,128)S(1)}, f32[2,256,256]{2,1,0:T(8,128)}, u32[]{:S(2)}) copy-start(f32[2,256,256]{2,1,0:T(8,128)} %param.5) | copy-start | bytes 1572868
  144.1 160.7 %all-gather.5.cloned.1.call-start = ((), (), s32[]{:S(2)}) async-start(), calls=%async_computation.3 | async-start | bytes 12681216 | tf_op jit(solution)/shard_map/all_gather | solution.py:24
  144.8 283.0 %all-reduce.7.cloned.1.call-start = ((), (), s32[]{:S(2)}) async-start(), calls=%async_computation.2 | async-start | bytes 3145728 | tf_op jit(solution)/shard_map/psum | solution.py:35
  238.6 2.2 copy-start
  247.4 281.6 %all-reduce.9.cloned.1.call-start = ((), (), s32[]{:S(2)}) async-start(), calls=%async_computation.4 | async-start | bytes 1572864 | tf_op jit(solution)/shard_map/psum | solution.py:33
  437.0 2.2 copy-start.1
  445.8 230.2 %all-reduce.11.cloned.1.call-start = ((), (), s32[]{:S(2)}) async-start(), calls=%async_computation.5 | async-start | bytes 3145728 | tf_op jit(solution)/shard_map/psum | solution.py:35
  542.5 2.2 copy-start.2
Sparse Core Ops, SparseCore 0:
  10.4 76.6 all-gather.2
  144.2 80.8 all-reduce.4
  228.3 76.4 all-gather.4
  307.1 120.6 all-reduce.6
  445.9 83.0 all-reduce.8
  551.3 124.6 all-reduce.10
where the time goes:
time: 703 us; the launch traced here: 694 us
  waiting for transfers between devices  508 us (72%)
  local copies, waits for them, and re-layouts  88.3 us (13%)
  matrix products  82.8 us (12%)
  between operations  14 us (2%)
    psum x2, waiting for transfers between devices, body(): image_sum = lax.psum(product(updated, column_vectors), 'col')  208 us
    psum x2, waiting for transfers between devices, body(): projected = lax.psum(partial_value, 'row')  163 us
    all_gather x2, waiting for transfers between devices, body(): lax.all_gather(sliver[None], ('row', 'col'), axis=0, tiled=True)  136 us
    dot_general x12, matrix products, product(): jnp.dot(factor_one, factor_two, precision=highest, preferred_element_type...  82.8 us
    unnamed x14, local copies, waits for them, and re-layouts  47.9 us
    reshape x2, local copies, waits for them, and re-layouts, body(): vectors = everything.reshape(row_count, col_count, rows_loc, piece_cols)  38.8 us
  transfers between devices with their start and end apart: 6, of which 6 were waited for; matrix products, arithmetic and copies ran while one was open for 9% of the time, Pallas kernels for 0%

commit v1 on v0

v1 whole, which is shorter than its diff:
```python
import jax
import jax.numpy as jnp
from jax import lax
from jax.sharding import PartitionSpec as P

HIGH = lax.Precision.HIGH


def mm(a, b, ca, cb):
    return lax.dot_general(a, b, (((ca,), (cb,)), ((), ())), precision=HIGH, preferred_element_type=jnp.float32)


def body(window, reflectors, factors):
    panels, rows, piece = reflectors.shape
    cols = window.shape[1]
    row_n = lax.axis_size("row")
    col_n = lax.axis_size("col")
    block = piece * col_n
    width = panels * block
    c = lax.axis_index("col")
    vt = jnp.swapaxes(reflectors, 1, 2)
    vr = lax.all_gather(vt, "col", axis=1, tiled=True).reshape(width, rows)
    halves = vt.reshape(panels, piece, 2, cols)
    k = c % 2
    own = lax.dynamic_index_in_dim(halves, k, 2, keepdims=False)
    other = lax.dynamic_index_in_dim(halves, 1 - k, 2, keepdims=False)
    pairs_a = []
    pairs_b = []
    for r in range(row_n):
        for cc in range(col_n):
            pairs_a.append((r * col_n + cc, (cc // 2) * col_n + 2 * r + cc % 2))
            pairs_b.append((r * col_n + cc, (cc // 2) * col_n + 2 * r + 1 - cc % 2))
    got_a = lax.ppermute(own, ("row", "col"), pairs_a)
    got_b = lax.ppermute(other, ("row", "col"), pairs_b)
    first = jnp.where(k == 0, got_a, got_b)
    second = jnp.where(k == 0, got_b, got_a)
    pair = jnp.stack([first, second], 1)
    vc = lax.all_gather(pair, "row", axis=1, tiled=True).reshape(width, cols)

    p_part = mm(vr, window, 1, 0)
    y_part = mm(window, vc, 1, 1)
    p_own = lax.psum_scatter(p_part, "row", scatter_dimension=0, tiled=True)
    y_own = lax.psum_scatter(y_part, "col", scatter_dimension=0, tiled=True)
    g12 = lax.psum(mm(vc[:block], vc[block:], 1, 1), "col")
    s_own = lax.psum(mm(p_own, vc, 1, 1), "col")
    t1, t2 = factors[0], factors[1]
    t12 = -mm(mm(t1, g12, 1, 0), t2, 1, 0)
    tc = jnp.concatenate([jnp.concatenate([t1, t12], 1), jnp.concatenate([jnp.zeros_like(t1), t2], 1)], 0)
    p_own = p_own - mm(mm(s_own, tc, 1, 0), vc, 1, 0)
    z_own = mm(y_own, tc, 1, 0)
    p_all = lax.all_gather(p_own, "row", axis=0, tiled=True)
    z_all = lax.all_gather(z_own, "col", axis=0, tiled=True)
    q = mm(tc, p_all, 0, 0)
    return window - mm(vr, q, 0, 0) - mm(z_all, vc, 1, 0)


def solution(mesh):
    placed = (P("row", "col"), P(None, "row", "col"), P())
    return jax.shard_map(body, mesh=mesh, in_specs=placed, out_specs=P("row", "col"), check_vma=False)
```

time: 703 us -> 485 us (0.69); the launches traced: 694 us -> 484 us
  waiting for transfers between devices: 508 us -> 403 us
  local copies, waits for them, and re-layouts: 88.3 us -> 19.6 us
  matrix products: 82.8 us -> 44.8 us
    psum x4 -> x1, waiting for transfers between devices: 371 us -> 106 us  [body(): s_own = lax.psum(mm(p_own, vc, 1, 1), 'col')]
    reduce_scatter x0 -> x1, waiting for transfers between devices: none -> 74.3 us  [body(): p_own = lax.psum_scatter(p_part, 'row', scatter_dimension=0, tiled=True)]
    unnamed x6 -> x8, waiting for transfers between devices: 0.76 us -> 61.7 us
    dot_general x12, matrix products: 82.8 us -> 44.8 us  [mm(): lax.dot_general(a, b, (((ca,), (cb,)), ((), ())), precision=HIGH, preferr...]
    reshape x2 -> x1, local copies, waits for them, and re-layouts: 38.8 us -> 1.05 us  [body(): halves = vt.reshape(panels, piece, 2, cols)]
    unnamed x14, local copies, waits for them, and re-layouts: 47.9 us -> 10.7 us
    all_gather x2 -> x4, waiting for transfers between devices: 136 us -> 161 us  [the longest x1 45.8 us: body(): p_all = lax.all_gather(p_own, 'row', axis=0, tiled=True)]
  transfers between devices with their start and end apart: 6 -> 9, of which waited for: 6 -> 8; matrix products, arithmetic and copies ran while one was open for 9% -> 10% of each run, Pallas kernels for 0% -> 0%
where the time goes in v1:
time: 485 us; the launch traced here: 484 us
  waiting for transfers between devices  403 us (83%)
  matrix products  44.8 us (9%)
  local copies, waits for them, and re-layouts  19.6 us (4%)
  between operations  13.6 us (3%)
    psum x1, waiting for transfers between devices, body(): s_own = lax.psum(mm(p_own, vc, 1, 1), 'col')  106 us
    reduce_scatter x1, waiting for transfers between devices, body(): p_own = lax.psum_scatter(p_part, 'row', scatter_dimension=0, tiled=True)  74.3 us
    unnamed x8, waiting for transfers between devices  61.7 us
    all_gather x1, waiting for transfers between devices, body(): p_all = lax.all_gather(p_own, 'row', axis=0, tiled=True)  45.8 us
    dot_general x12, matrix products, mm(): lax.dot_general(a, b, (((ca,), (cb,)), ((), ())), precision=HIGH, preferr...  44.8 us
    all_gather x1, waiting for transfers between devices, body(): vr = lax.all_gather(vt, 'col', axis=1, tiled=True).reshape(width, rows)  44.7 us
    all_gather x1, waiting for transfers between devices, body(): vc = lax.all_gather(pair, 'row', axis=1, tiled=True).reshape(width, cols)  42.1 us
    all_gather x1, waiting for transfers between devices, body(): z_all = lax.all_gather(z_own, 'col', axis=0, tiled=True)  28.2 us
  transfers between devices with their start and end apart: 9, of which 8 were waited for; matrix products, arithmetic and copies ran while one was open for 10% of the time, Pallas kernels for 0%

profile of v1, /device:TPU:1, one launch (start us, length us, event | category | flops | bytes accessed | tf_op | source)
XLA Modules:
  0.0 484.4 jit_solution(11163545829636249357)
XLA Ops:
  6.5 0.7 all-gather.7.cloned.1.call-update
  7.3 1.1 reshape.11
  8.4 0.2 constant_dynamic-slice_fusion.1
  8.6 1.5 collective-permute-start.1
  10.1 0.7 collective-permute-start
  10.7 0.3 collective-permute-done.1
  11.0 0.7 pad_maximum_fusion
  11.8 44.7 %all-gather.7.cloned.1.call-done = f32[2,256,1536]{2,1,0:T(8,128)} async-done(((f32[2,16,1536]{2,1,0:T(8,128)}), f32[2,256,1536]{2,1,0:T(8,128)}) %all-gather.7.cloned.1.call-update) | async-done | bytes 3145744 | tf_op jit(solution)/shard_map/all_gather | solution.py:22
  56.5 8.5 %fusion.21 = f32[512,768]{1,0:T(8,128)} fusion(f32[512,1536]{1,0:T(8,128)} %bitcast.55, f32[1536,768]{1,0:T(8,128)} %param.3), kind=kOutput, calls=%fused_computation.34 | convolution fusion | flops 3623878656 | bytes 9437184 | tf_op jit(solution)/shard_map/dot_general | solution.py:10
  65.1 42.1 %all-gather.5.cloned.1.call-done = f32[2,16,16,768]{3,2,1,0:T(8,128)} async-done(((f32[2,2,16,768]{3,2,1,0:T(8,128)}), f32[2,16,16,768]{3,2,1,0:T(8,128)}) %all-gather.5.cloned.1.call-update) | async-done | bytes 1572880 | tf_op jit(solution)/shard_map/all_gather | solution.py:38
  107.1 1.6 fusion.18
  108.7 1.2 fusion.20
  110.0 74.3 %reduce-scatter.5.cloned.1.call-done = f32[64,768]{1,0:T(8,128)} async-done(((f32[512,768]{1,0:T(8,128)}), f32[64,768]{1,0:T(8,128)}) %reduce-scatter.5.cloned.1.call-update) | async-done | bytes 196624 | tf_op jit(solution)/shard_map/reduce_scatter | solution.py:42
  184.3 2.4 fusion.22
  186.8 7.9 %convolution_bitcast_fusion = f32[1536,512]{0,1:T(8,128)} fusion(f32[512,768]{1,0:T(8,128)S(1)} %bitcast.52, f32[1536,768]{1,0:T(8,128)} %param.3), kind=kOutput, calls=%fused_computation.2 | convolution fusion | flops 3623878656 | bytes 9437184 | tf_op jit(solution)/shard_map/dot_general | solution.py:10
  194.7 3.6 copy.26
  198.3 0.2 all-gather.9.cloned.1.call-start
  198.5 0.8 copy-done.2
  199.6 106.0 %all-reduce.4.cloned.1.call-done = (f32[64,512]{1,0:T(8,128)}, f32[256,256]{1,0:T(8,128)}) async-done(((f32[64,512]{1,0:T(8,128)}, f32[256,256]{1,0:T(8,128)}), (f32[64,512]{1,0:T(8,128)}, f32[256,256]{1,0:T(8,128)})) %all-reduce.4.cloned.1.call-update) | async-done | bytes 393232 | tf_op jit(solution)/shard_map/psum | solution.py:45
  305.6 1.3 fusion.5
  307.0 0.4 convolution_negate_fusion
  307.4 1.4 fusion.3
  308.8 1.3 convolution_subtract_fusion
  310.1 60.9 %reduce-scatter.7.cloned.1.call-done = f32[96,512]{1,0:T(8,128)} async-done(((f32[1536,512]{1,0:T(8,128)}), f32[96,512]{1,0:T(8,128)}) %reduce-scatter.7.cloned.1.call-update) | async-done | bytes 196624
  371.0 2.1 fusion.1
  373.2 6.0 %copy.22 = f32[1536,768]{0,1:T(8,128)} copy(f32[1536,768]{1,0:T(8,128)} %param.3) | data formatting | bytes 9437184 | tf_op args[0]
  379.2 45.8 %all-gather.9.cloned.1.call-done = f32[512,768]{1,0:T(8,128)} async-done(((f32[64,768]{1,0:T(8,128)}), f32[512,768]{1,0:T(8,128)}) %all-gather.9.cloned.1.call-update) | async-done | bytes 1572880 | tf_op jit(solution)/shard_map/all_gather | solution.py:51
  425.0 3.0 fusion.2
  428.1 6.3 %fusion.23 = f32[768,1536]{1,0:T(8,128)} fusion(f32[512,768]{1,0:T(8,128)S(1)} %fusion.2, f32[512,1536]{1,0:T(8,128)S(1)} %bitcast.56), kind=kOutput, calls=%fused_computation.36 | convolution fusion | flops 3623878656 | bytes 9437184 | tf_op jit(solution)/shard_map/dot_general | solution.py:10
  434.3 28.2 %all-gather.11.cloned.1.call-done = f32[1536,512]{1,0:T(8,128)} async-done(((f32[96,512]{1,0:T(8,128)}), f32[1536,512]{1,0:T(8,128)}) %all-gather.11.cloned.1.call-update) | async-done | bytes 3145744 | tf_op jit(solution)/shard_map/all_gather | solution.py:52
  462.5 9.0 %fusion = f32[1536,768]{0,1:T(8,128)} fusion(f32[1536,768]{0,1:T(8,128)} %copy.22, f32[768,1536]{1,0:T(8,128)} %fusion.23, f32[1536,512]{1,0:T(8,128)} %all-gather.11.cloned.1.call-done, f32[512,768]{1,0:T(8,128)S(1)} %bitcast.54), kind=kOutput, calls=%fused_computation.1 | convolution fusion | flops 3626237952 | bytes 18874368 | tf_op jit(solution)/shard_map/dot_general | solution.py:10
  471.5 6.0 %copy.24 = f32[1536,768]{1,0:T(8,128)} copy(f32[1536,768]{0,1:T(8,128)} %fusion) | data formatting | bytes 9437184 | tf_op jit(solution)/shard_map/sub | solution.py:54
  (26 shorter events, 0.6 us)
Async XLA Ops:
  6.5 49.9 %all-gather.7.cloned.1.call-start = ((), (), s32[]{:S(2)}) async-start(), calls=%async_computation.3 | async-start | bytes 3342336 | tf_op jit(solution)/shard_map/all_gather | solution.py:22
  7.3 99.9 %all-gather.5.cloned.1.call-start = ((), (), s32[]{:S(2)}) async-start(), calls=%async_computation.2 | async-start | bytes 1769472 | tf_op jit(solution)/shard_map/all_gather | solution.py:38
  8.6 2.4 collective-permute-start.1
  10.1 0.9 collective-permute-start
  11.7 172.5 %reduce-scatter.5.cloned.1.call-start = ((), (), s32[]{:S(2)}) async-start(), calls=%async_computation.4 | async-start | bytes 1769472 | tf_op jit(solution)/shard_map/reduce_scatter | solution.py:42
  65.0 240.6 %all-reduce.4.cloned.1.call-start = ((), (), s32[]{:S(2)}) async-start(), calls=%async_computation.8 | async-start | bytes 786432 | tf_op jit(solution)/shard_map/psum | solution.py:45
  107.1 77.2 %copy-start = (f32[2,16,16,768]{3,2,1,0:T(8,128)S(1)}, f32[2,16,16,768]{3,2,1,0:T(8,128)}, u32[]{:S(2)}) copy-start(f32[2,16,16,768]{3,2,1,0:T(8,128)} %all-gather.5.cloned.1.call-done) | copy-start | bytes 4718596
  186.7 184.3 %reduce-scatter.7.cloned.1.call-start = ((), (), s32[]{:S(2)}) async-start(), calls=%async_computation.7 | async-start | bytes 3342336
  198.3 1.0 copy-start.2
  198.3 110.5 %copy-start.3 = (f32[64,768]{1,0:T(8,128)S(1)}, f32[64,768]{1,0:T(8,128)}, u32[]{:S(2)}) copy-start(f32[64,768]{1,0:T(8,128)} %reduce-scatter.5.cloned.1.call-done) | copy-start | bytes 589828
  198.3 226.7 %all-gather.9.cloned.1.call-start = ((), (), s32[]{:S(2)}) async-start(), calls=%async_computation.5 | async-start | bytes 1769472 | tf_op jit(solution)/shard_map/all_gather | solution.py:51
  310.1 152.4 %all-gather.11.cloned.1.call-start = ((), (), s32[]{:S(2)}) async-start(), calls=%async_computation.6 | async-start | bytes 3342336 | tf_op jit(solution)/shard_map/all_gather | solution.py:52
  425.0 3.0 copy-start.1
Sparse Core Ops, SparseCore 0:
  9.0 47.4 all-gather.6
  58.8 48.2 all-gather.4
  110.9 73.3 reduce-scatter.4
  186.9 118.7 all-reduce.3
  307.9 63.0 reduce-scatter.6
  373.2 51.7 all-gather.8
  426.7 35.7 all-gather.10

commit v2 on v0

v2 whole, which is shorter than its diff:
```python
import jax
import jax.numpy as jnp
from jax import lax
from jax.experimental import pallas as pl
from jax.experimental.pallas import tpu as pltpu
from jax.sharding import PartitionSpec as P

MESH = pl.DeviceIdType.MESH
F32 = jnp.float32
HIGH = lax.Precision.HIGH


def mm(a, b, ca, cb):
    return lax.dot_general(a, b, (((ca,), (cb,)), ((), ())), precision=HIGH, preferred_element_type=F32)


def remote(src, dst, ssem, rsem, dev):
    return pltpu.make_async_remote_copy(
        src_ref=src, dst_ref=dst, send_sem=ssem, recv_sem=rsem, device_id=dev, device_id_type=MESH
    )


def landed(ref, sem):
    pltpu.make_async_copy(ref, ref, sem).wait()


class Gather:
    def __init__(self, own, place, ring, pair, core, ssem, rsem):
        self.own, self.place, self.ring, self.pair, self.core = own, place, ring, pair, core
        self.ssem, self.rsem, self.started = ssem, rsem, []

    def send(self, src, dst, slot, dev):
        copy = remote(src, dst, self.ssem.at[len(self.started)], self.rsem.at[slot], dev)
        copy.start()
        self.started.append(copy)

    def start(self):
        place = self.place(0, 0, 0)
        self.send(self.own, place, 4, self.pair)
        for d in (1, 3, 2):
            self.send(self.own, place, d, self.ring(d))
        if self.core is not None:
            self.send(self.own, place, 8, self.core)

    def wait(self, level, d, other=0):
        landed(self.place(level, d, other), self.rsem.at[other * 8 + level * 4 + d])

    def to_core(self, level, d):
        place = self.place(level, d, 0)
        self.send(place, place, 8 + level * 4 + d, self.core)

    def relay_pair(self):
        self.wait(1, 0)
        place = self.place(1, 0, 0)
        for d in (1, 3, 2):
            self.send(place, place, 4 + d, self.ring(d))
        if self.core is not None:
            self.to_core(1, 0)

    def take_ring(self, level):
        for d in (1, 3, 2):
            self.wait(level, d)
            if self.core is not None:
                self.to_core(level, d)

    def take_core(self, level):
        for d in (0, 1, 3, 2):
            self.wait(level, d, 1)

    def finish(self):
        for copy in self.started:
            copy.wait_send()


def kernel(
    w_hbm, v_hbm, t_hbm, out_hbm,
    w, vr, vc, tf, tc, vv,
    p, p_rx, p_acc, p_pair, p_own, p_all,
    y_send, y_core, y_own, y_rx, y_acc, y_pair, z_all,
    g_part, g_rx, g_own, g_all, s_part, s_rx, s_own, s_all,
    load_sem, zero_s, zero_r, vr_s, vr_r, vc_s, vc_r, pa_s, pa_r, za_s, za_r,
    p_s, p_r, pz_s, pz_r, yc_s, yc_r, y_s, y_r, yz_s, yz_r,
    g_s, g_r, out_sem,
):
    r = lax.axis_index("row")
    c = lax.axis_index("col")
    x, zh = r // 2, r % 2
    zl, y, k = c // 8, (c // 2) % 4, c % 2

    def dev(x_, zh_, zl_, y_, k_):
        return (x_ * 2 + zh_, (zl_ * 4 + y_) * 2 + k_)

    def ring_x(d):
        return dev((x + d) % 4, zh, zl, y, k)

    def ring_y(d):
        return dev(x, zh, zl, (y + d) % 4, k)

    pair_x = dev(x, 1 - zh, zl, y, k)
    pair_y = dev(x, zh, 1 - zl, y, k)
    core = dev(x, zh, zl, y, 1 - k)

    def level_of(z, level):
        return z if level == 0 else 1 - z

    def col_index(level, d, other):
        return (level_of(zl, level) * 4 + (y + 4 - d) % 4) * 2 + level_of(k, other)

    def row_index(level, d):
        return ((x + 4 - d) % 4) * 2 + level_of(zh, level)

    def z_index(level, d, other):
        return level_of(k, other) * 8 + level_of(zl, level) * 4 + (y + 4 - d) % 4

    gather_vr = Gather(v_hbm, lambda l, d, o: vr.at[:, col_index(l, d, o)], ring_y, pair_y, core, vr_s, vr_r)
    gather_vr.start()
    halves = []
    for h in range(2):
        src = v_hbm.at[:, :, pl.ds(h * 768, 768)]
        at_home = jnp.logical_and(c // 2 == r, k == h)
        away = jnp.logical_not(at_home)
        local = pltpu.make_async_copy(src, vc.at[:, c], zero_r.at[k])
        far = remote(src, vc.at[:, c], zero_s.at[h], zero_r.at[k], (c // 2, 2 * r + h))
        pl.when(at_home)(local.start)
        pl.when(away)(far.start)
        halves.append((away, far))
    own_v = pltpu.make_async_copy(v_hbm, vr.at[:, c], load_sem.at[0])
    own_v.start()
    load_w = pltpu.make_async_copy(w_hbm, w, load_sem.at[1])
    load_w.start()
    load_t = pltpu.make_async_copy(t_hbm, tf, load_sem.at[2])
    load_t.start()

    mine = vc.at[:, pl.ds(2 * r, 2)]
    gather_vc = Gather(
        mine, lambda l, d, o: vc.at[:, pl.ds(2 * row_index(l, d), 2)], ring_x, pair_x, None, vc_s, vc_r
    )
    gather_vr.relay_pair()
    for kk in range(2):
        landed(vc.at[:, 2 * r + kk], zero_r.at[kk])
    gather_vc.start()
    gather_vr.take_ring(0)
    gather_vc.relay_pair()
    own_v.wait()
    load_w.wait()
    load_t.wait()
    gather_vr.take_ring(1)
    gather_vr.take_core(0)
    gather_vr.take_core(1)

    g_part[...] = mm(vr[0, c], vr[1].reshape(256, 1536), 1, 1)

    def g_send(i, _):
        pltpu_copy = remote(g_part, g_rx.at[i], g_s.at[0], g_r.at[0], ((r + 1 + i) % 8, c))
        pltpu_copy.start()
        return 0

    lax.fori_loop(0, 7, g_send, 0)
    p_copies = []
    for n in range(3):
        p[n] = mm(vr[...].reshape(512, 1536), w[:, n * 256:(n + 1) * 256], 1, 0).reshape(4, 2, 64, 256)
        for d in (2, 1, 3):
            copy = remote(
                p.at[n, (x + d) % 4], p_rx.at[n, d - 1], p_s.at[n, d - 1], p_r.at[n, d - 1], ring_x(d)
            )
            copy.start()
            p_copies.append(copy)

    gather_vc.take_ring(0)
    gather_vc.take_ring(1)

    def y_tile(row):
        rows = pl.ds(pl.multiple_of(row, 384), 384)
        return mm(w[rows, :], vc[...].reshape(512, 768), 1, 1)

    y_copies = []
    for t in range(2):
        y_send[t] = y_tile((1 - k) * 768 + t * 384)
        copy = remote(y_send.at[t], y_core.at[t], yc_s.at[t], yc_r.at[t], core)
        copy.start()
        y_copies.append(copy)
    for t in range(2):
        part = y_tile(k * 768 + t * 384)
        landed(y_core.at[t], yc_r.at[t])
        y_own[t] = (part + y_core[t]).reshape(4, 96, 512)
        for d in (2, 1, 3):
            copy = remote(
                y_own.at[t, (y + d) % 4], y_rx.at[t, d - 1], y_s.at[t, d - 1], y_r.at[t, d - 1], ring_y(d)
            )
            copy.start()
            y_copies.append(copy)

    landed(g_rx, g_r.at[0])
    g_own[...] = (g_part[...] + g_rx[0] + g_rx[1] + g_rx[2]) + (g_rx[3] + g_rx[4] + g_rx[5] + g_rx[6])
    g_all[c] = g_own[...]

    def g_spread(i, _):
        remote(g_own, g_all.at[c], g_s.at[1], g_r.at[1], (r, (c + 1 + i) % 16)).start()
        return 0

    lax.fori_loop(0, 15, g_spread, 0)

    for n in range(3):
        for d in range(3):
            landed(p_rx.at[n, d], p_r.at[n, d])
        p_acc[n] = (p[n, x] + p_rx[n, 0]) + (p_rx[n, 1] + p_rx[n, 2])
        copy = remote(p_acc.at[n, 1 - zh], p_pair.at[n], pz_s.at[n], pz_r.at[n], pair_x)
        copy.start()
        p_copies.append(copy)
    for n in range(3):
        landed(p_pair.at[n], pz_r.at[n])
        p_own[:, n * 256:(n + 1) * 256] = p_acc[n, zh] + p_pair[n]

    part = mm(p_own[...], vc[...].reshape(512, 768), 1, 1)
    s_part[0] = part[:, :256]
    s_part[1] = part[:, 256:]

    def chunk(ref, who):
        return ref.at[who % 2, pl.ds(pl.multiple_of(who // 2 * 8, 8), 8)]

    def s_send(i, _):
        to = (c + 1 + i) % 16
        remote(chunk(s_part, to), s_rx.at[i], g_s.at[2], g_r.at[2], (r, to)).start()
        return 0

    lax.fori_loop(0, 15, s_send, 0)

    for t in range(2):
        for d in range(3):
            landed(y_rx.at[t, d], y_r.at[t, d])
        y_acc[t] = (y_own[t, y] + y_rx[t, 0]) + (y_rx[t, 1] + y_rx[t, 2])
    copy = remote(y_acc.at[1 - zl], y_pair, yz_s.at[0], yz_r.at[0], pair_y)
    copy.start()
    y_copies.append(copy)

    landed(s_rx, g_r.at[2])
    total = s_part[k, pl.ds(pl.multiple_of(c // 2 * 8, 8), 8)]
    for i in range(15):
        total = total + s_rx[i]
    s_own[...] = total
    s_all[k, pl.ds(pl.multiple_of(c // 2 * 8, 8), 8)] = total

    def s_spread(i, _):
        remote(s_own, chunk(s_all, c), g_s.at[3], g_r.at[3], (r, (c + 1 + i) % 16)).start()
        return 0

    lax.fori_loop(0, 15, s_spread, 0)

    landed(g_all.at[pl.ds(0, 15)], g_r.at[1])
    tc[0:256, 0:256] = tf[0]
    tc[256:512, 256:512] = tf[1]
    tc[256:512, 0:256] = jnp.zeros((256, 256), F32)
    tc[0:256, 256:512] = -mm(mm(tf[0], g_all[...].reshape(256, 256), 1, 0), tf[1], 1, 0)

    landed(y_pair, yz_r.at[0])
    z_place = lambda l, d, o: z_all.at[z_index(l, d, o)]
    z_all[z_index(0, 0, 0)] = mm(y_acc[zl] + y_pair[...], tc[...], 1, 0)
    gather_z = Gather(z_place(0, 0, 0), z_place, ring_y, pair_y, core, za_s, za_r)
    gather_z.start()

    landed(s_rx, g_r.at[3])
    s_rows = jnp.concatenate([s_all[0], s_all[1]], axis=1)
    p_all[r] = p_own[...] - mm(mm(s_rows, tc[...], 1, 0), vc[...].reshape(512, 768), 1, 0)
    p_place = lambda l, d, o: p_all.at[row_index(l, d)]
    gather_p = Gather(p_place(0, 0, 0), p_place, ring_x, pair_x, None, pa_s, pa_r)
    gather_p.start()

    def vv_tile(i):
        cols = slice(i * 512, (i + 1) * 512)
        vv[:, cols] = mm(tc[...], vr[...].reshape(512, 1536)[:, cols], 1, 0)

    gather_z.relay_pair()
    gather_p.relay_pair()
    for i in range(3):
        vv_tile(i)

    def z_tile(level, other):
        first = level_of(k, other) * 8 + level_of(zl, level) * 4
        rows = pl.ds(pl.multiple_of(first * 96, 384), 384)
        w[rows, :] = w[rows, :] - mm(z_all[pl.ds(first, 4)].reshape(384, 512), vc[...].reshape(512, 768), 1, 0)

    gather_z.take_ring(0)
    z_tile(0, 0)
    gather_z.take_ring(1)
    z_tile(1, 0)
    gather_z.take_core(0)
    z_tile(0, 1)
    gather_z.take_core(1)
    z_tile(1, 1)
    gather_p.take_ring(0)
    gather_p.take_ring(1)

    outs = []
    for i in range(4):
        rows = slice(i * 384, (i + 1) * 384)
        w[rows, :] = w[rows, :] - mm(vv[:, rows], p_all[...].reshape(512, 768), 0, 0)
        copy = pltpu.make_async_copy(w.at[pl.ds(i * 384, 384)], out_hbm.at[pl.ds(i * 384, 384)], out_sem.at[i])
        copy.start()
        outs.append(copy)

    for away, far in halves:
        pl.when(away)(far.wait_send)
    for gather in (gather_vr, gather_vc, gather_z, gather_p):
        gather.finish()
    for copy in p_copies + y_copies:
        copy.wait_send()
    landed(g_rx, g_s.at[0])
    landed(g_all.at[pl.ds(0, 15)], g_s.at[1])
    landed(s_rx, g_s.at[2])
    landed(s_rx, g_s.at[3])
    for copy in outs:
        copy.wait()


def body(window, reflectors, factors):
    vt = jnp.swapaxes(reflectors, 1, 2)
    dma = pltpu.SemaphoreType.DMA
    vmem = lambda *s: pltpu.VMEM(s, F32)
    return pl.pallas_call(
        kernel,
        out_shape=jax.ShapeDtypeStruct(window.shape, F32),
        in_specs=[pl.BlockSpec(memory_space=pl.ANY)] * 3,
        out_specs=pl.BlockSpec(memory_space=pl.ANY),
        scratch_shapes=[
            vmem(1536, 768), vmem(2, 16, 16, 1536), vmem(2, 16, 16, 768), vmem(2, 256, 256), vmem(512, 512),
            vmem(512, 1536),
            vmem(3, 4, 2, 64, 256), vmem(3, 3, 2, 64, 256), vmem(3, 2, 64, 256), vmem(3, 64, 256), vmem(64, 768),
            vmem(8, 64, 768),
            vmem(2, 384, 512), vmem(2, 384, 512), vmem(2, 4, 96, 512), vmem(2, 3, 96, 512), vmem(2, 96, 512),
            vmem(96, 512), vmem(16, 96, 512),
            vmem(16, 256), vmem(7, 16, 256), vmem(16, 256), vmem(16, 16, 256),
            vmem(2, 64, 256), vmem(15, 8, 256), vmem(8, 256), vmem(2, 64, 256),
            dma((3,)), dma((2,)), dma((2,)), dma((15,)), dma((16,)), dma((7,)), dma((8,)), dma((7,)), dma((8,)),
            dma((15,)), dma((16,)),
            dma((3, 3)), dma((3, 3)), dma((3,)), dma((3,)), dma((2,)), dma((2,)), dma((2, 3)), dma((2, 3)),
            dma((1,)), dma((1,)),
            dma((4,)), dma((4,)), dma((4,)),
        ],
        compiler_params=pltpu.CompilerParams(has_side_effects=True, vmem_limit_bytes=60 * 1024 * 1024),
    )(window, vt, factors)


def solution(mesh):
    placed = (P("row", "col"), P(None, "row", "col"), P())
    return jax.shard_map(body, mesh=mesh, in_specs=placed, out_specs=P("row", "col"), check_vma=False)
```

time: 703 us -> 126 us (0.18); the launches traced: 694 us -> 126 us
  waiting for transfers between devices: 508 us -> 0 us
  Pallas kernels: 0 us -> 121 us
  local copies, waits for them, and re-layouts: 88.3 us -> 4.83 us
  matrix products: 82.8 us -> 0 us
  between operations: 14 us -> 0.01 us
    psum x4 -> x0, waiting for transfers between devices: 371 us -> none  [the longest x2 208 us: body(): image_sum = lax.psum(product(updated, column_vectors), 'col')]
    all_gather x2 -> x0, waiting for transfers between devices: 136 us -> none  [body(): lax.all_gather(sliver[None], ('row', 'col'), axis=0, tiled=True)]
    pallas_call x0 -> x1, Pallas kernels: none -> 121 us  [body(): pl.pallas_call(kernel, out_shape=jax.ShapeDtypeStruct(window.shape, F32),...]
    dot_general x12 -> x0, matrix products: 82.8 us -> none  [product(): jnp.dot(factor_one, factor_two, precision=highest, preferred_element_type...]
    unnamed x14 -> x1, local copies, waits for them, and re-layouts: 47.9 us -> 4.83 us
    reshape x2 -> x0, local copies, waits for them, and re-layouts: 38.8 us -> none  [body(): vectors = everything.reshape(row_count, col_count, rows_loc, piece_cols)]
  transfers between devices with their start and end apart: 6 -> 0, of which waited for: 6 -> 0; matrix products, arithmetic and copies ran while one was open for 9% -> 0% of each run, Pallas kernels for 0% -> 0%
where the time goes in v2:
time: 126 us
  Pallas kernels  121 us (96%)
  local copies, waits for them, and re-layouts  4.83 us (4%)
    pallas_call x1, Pallas kernels, body(): pl.pallas_call(kernel, out_shape=jax.ShapeDtypeStruct(window.shape, F32),...  121 us
    unnamed x1, local copies, waits for them, and re-layouts  4.83 us

profile of v2, /device:TPU:1, one launch (start us, length us, event | category | flops | bytes accessed | tf_op | source)
XLA Modules:
  0.0 126.2 jit_solution(16335862013751050035)
XLA Ops:
  0.0 121.3 %shard_map.37 = f32[1536,768]{1,0:T(8,128)} custom-call(f32[1536,768]{1,0:T(8,128)} %w_hbm.1, f32[2,16,1536]{2,1,0:T(8,128)} %bitcast.1, f32[2,256,256]{2,1,0:T(8,128)} %t_hbm.1), custom_call_target="tpu_custom_call" | custom-call | tf_op jit(solution)/shard_map/pallas_call | solution.py:319
  121.3 4.8 %copy.5 = f32[1536,768]{1,0:T(8,128)} copy(f32[1536,768]{1,0:T(8,128)} %shard_map.37) | data formatting | bytes 9437184

commit v3 on v2

v3 whole, which is shorter than its diff:
```python
import jax
import jax.numpy as jnp
from jax import lax
from jax.experimental import pallas as pl
from jax.experimental.pallas import tpu as pltpu
from jax.sharding import PartitionSpec as P

MESH = pl.DeviceIdType.MESH
F32 = jnp.float32
HIGH = lax.Precision.HIGH


def mm(a, b, ca, cb):
    return lax.dot_general(a, b, (((ca,), (cb,)), ((), ())), precision=HIGH, preferred_element_type=F32)


def remote(src, dst, ssem, rsem, dev):
    return pltpu.make_async_remote_copy(
        src_ref=src, dst_ref=dst, send_sem=ssem, recv_sem=rsem, device_id=dev, device_id_type=MESH
    )


def landed(ref, sem):
    pltpu.make_async_copy(ref, ref, sem).wait()


class Sends:
    def __init__(self, ssem):
        self.ssem, self.started = ssem, []

    def __call__(self, src, dst, rsem, dev):
        copy = remote(src, dst, self.ssem.at[len(self.started)], rsem, dev)
        copy.start()
        self.started.append(copy)

    def finish(self):
        for copy in self.started:
            copy.wait_send()


class Gather:
    def __init__(self, own, place, ring, pair, core, send, rsem):
        self.own, self.place, self.ring, self.pair, self.core = own, place, ring, pair, core
        self.send, self.rsem = send, rsem

    def sem(self, level, d, q, other=0):
        return self.rsem.at[other * 16 + level * 8 + d * 2 + q]

    def start(self):
        for q in (0, 1):
            self.send(self.own(q), self.place(0, 0, 0, q), self.sem(1, 0, q), self.pair)
            self.send(self.own(q), self.place(0, 0, 0, q), self.sem(0, 1, q), self.ring(1))
            self.send(self.own(1 - q), self.place(0, 0, 0, 1 - q), self.sem(0, 3, 1 - q), self.ring(3))
        if self.core is not None:
            for q in (0, 1):
                self.send(self.own(q), self.place(0, 0, 0, q), self.sem(0, 0, q, 1), self.core)

    def wait(self, level, d, q, other=0):
        landed(self.place(level, d, other, q), self.sem(level, d, q, other))

    def to_core(self, level, d, q):
        if self.core is not None:
            place = self.place(level, d, 0, q)
            self.send(place, place, self.sem(level, d, q, 1), self.core)

    def hand_on(self, level):
        for d, q, to in ((1, 0, 1), (3, 1, 3)):
            self.wait(level, d, q)
            place = self.place(level, d, 0, q)
            self.send(place, place, self.sem(level, 2, q), self.ring(to))
            self.to_core(level, d, q)

    def relay_pair(self):
        for q in (0, 1):
            self.wait(1, 0, q)
            place = self.place(1, 0, 0, q)
            self.send(place, place, self.sem(1, 1, q), self.ring(1))
            self.send(place, place, self.sem(1, 3, q), self.ring(3))
            self.to_core(1, 0, q)

    def take_near(self, level):
        for d, q in ((1, 1), (3, 0)):
            self.wait(level, d, q)
            self.to_core(level, d, q)

    def take_far(self, level):
        for q in (0, 1):
            self.wait(level, 2, q)
            self.to_core(level, 2, q)

    def take_core(self, level):
        for d in (0, 1, 3, 2):
            for q in (0, 1):
                self.wait(level, d, q, 1)


def kernel(
    w_hbm, v_hbm, t_hbm, w, vv, p_all,
    vr, vc, tf, tc,
    p, p_far, p_rx, p_acc, p_pair, p_own,
    y_send, y_core, y_own, y_far, y_rx, y_acc, y_pair, z_all,
    g_part, g_rx, g_own, g_all, s_part, s_rx, s_own, s_all,
    load_sem, zero_s, zero_r, all_s, vr_r, vc_r, pa_r, za_r,
    pf_r, p_r, pz_r, yc_r, yf_r, y_r, yz_r, g_s, g_r,
):
    r = lax.axis_index("row")
    c = lax.axis_index("col")
    x, zh = r // 2, r % 2
    zl, y, k = c // 8, (c // 2) % 4, c % 2

    def dev(x_, zh_, zl_, y_, k_):
        return (x_ * 2 + zh_, (zl_ * 4 + y_) * 2 + k_)

    def ring_x(d):
        return dev((x + d) % 4, zh, zl, y, k)

    def ring_y(d):
        return dev(x, zh, zl, (y + d) % 4, k)

    pair_x = dev(x, 1 - zh, zl, y, k)
    pair_y = dev(x, zh, 1 - zl, y, k)
    core = dev(x, zh, zl, y, 1 - k)

    def level_of(z, level):
        return z if level == 0 else 1 - z

    def col_index(level, d, other):
        return (level_of(zl, level) * 4 + (y + 4 - d) % 4) * 2 + level_of(k, other)

    def row_index(level, d):
        return ((x + 4 - d) % 4) * 2 + level_of(zh, level)

    def vc_pair(level, d):
        other_x = (x + 4 - d) % 4
        return (level_of(zh, level) + c // 2) % 2 * 4 + (other_x + 4 - c // 4) % 4

    def z_index(level, d, other):
        return level_of(k, other) * 8 + level_of(zl, level) * 4 + (y + 4 - d) % 4

    load_w = pltpu.make_async_copy(w_hbm, w, load_sem.at[1])
    load_w.start()
    own_v = pltpu.make_async_copy(v_hbm, vr.at[:, c], load_sem.at[0])
    own_v.start()
    load_t = pltpu.make_async_copy(t_hbm, tf, load_sem.at[2])
    load_t.start()

    target = (x + y) % 4 * 2 + (zh + zl) % 2
    share = vc_pair(0, 0)
    barrier = pltpu.get_barrier_semaphore()

    def greet(device):
        pl.semaphore_signal(barrier, inc=1, device_id=device, device_id_type=MESH)

    for h in range(2):
        apart = jnp.logical_not(jnp.logical_and(target == r, 2 * r + h == c))
        pl.when(apart)(lambda h=h: greet((target, 2 * r + h)))
        apart = jnp.logical_not(jnp.logical_and(c // 2 == r, 2 * share + h == c))
        pl.when(apart)(lambda h=h: greet((c // 2, 2 * share + h)))
    for device in (ring_x(1), ring_x(3), ring_y(1), ring_y(3), pair_x, pair_y, core):
        greet(device)
    home = jnp.logical_and(r == 0, c // 2 == 0)
    pl.semaphore_wait(barrier, 11 - 2 * home.astype(jnp.int32))

    halves = []
    for h in range(2):
        src = v_hbm.at[:, :, pl.ds(h * 768, 768)]
        at_home = jnp.logical_and(target == r, 2 * r + h == c)
        away = jnp.logical_not(at_home)
        local = pltpu.make_async_copy(src, vc.at[:, c], zero_r.at[k])
        far = remote(src, vc.at[:, c], zero_s.at[h], zero_r.at[k], (target, 2 * r + h))
        pl.when(at_home)(local.start)
        pl.when(away)(far.start)
        halves.append((away, far))
    send = Sends(all_s)
    gather_vr = Gather(
        lambda q: v_hbm.at[q], lambda l, d, o, q: vr.at[q, col_index(l, d, o)], ring_y, pair_y, core, send, vr_r
    )
    gather_vr.start()
    vc_place = lambda l, d, o, q: vc.at[q, pl.ds(2 * vc_pair(l, d), 2)]
    gather_vc = Gather(lambda q: vc_place(0, 0, 0, q), vc_place, ring_x, pair_x, None, send, vc_r)

    gather_vr.hand_on(0)
    for kk in range(2):
        landed(vc.at[:, 2 * share + kk], zero_r.at[kk])
    gather_vc.start()
    gather_vr.relay_pair()
    gather_vr.take_near(0)
    gather_vc.hand_on(0)
    gather_vr.hand_on(1)
    gather_vr.take_far(0)
    gather_vc.relay_pair()
    own_v.wait()
    load_w.wait()
    load_t.wait()
    gather_vr.take_near(1)
    gather_vr.take_core(0)

    def p_tile(m):
        rows = vr[:, pl.ds(level_of(zl, m) * 8, 8)].reshape(256, 1536)
        p[m] = mm(rows, w[...], 1, 0).reshape(4, 2, 32, 768)
        right, left, far = (x + 1) % 4, (x + 3) % 4, (x + 2) % 4
        send(p.at[m, far, 0], p_far.at[m, 0], pf_r.at[m, 0], ring_x(1))
        send(p.at[m, far, 1], p_far.at[m, 1], pf_r.at[m, 1], ring_x(3))
        send(p.at[m, right, 1], p_rx.at[m, 0], p_r.at[m, 0], ring_x(1))
        send(p.at[m, left, 0], p_rx.at[m, 1], p_r.at[m, 1], ring_x(3))

    def p_hand_on(m):
        right, left = (x + 1) % 4, (x + 3) % 4
        landed(p_far.at[m, 0], pf_r.at[m, 0])
        p[m, right, 0] = p[m, right, 0] + p_far[m, 0]
        send(p.at[m, right, 0], p_rx.at[m, 2], p_r.at[m, 2], ring_x(1))
        landed(p_far.at[m, 1], pf_r.at[m, 1])
        p[m, left, 1] = p[m, left, 1] + p_far[m, 1]
        send(p.at[m, left, 1], p_rx.at[m, 3], p_r.at[m, 3], ring_x(3))

    def p_sum(m):
        for i in range(4):
            landed(p_rx.at[m, i], p_r.at[m, i])
        p_acc[m, 0] = p[m, x, 0] + (p_rx[m, 1] + p_rx[m, 2])
        p_acc[m, 1] = p[m, x, 1] + (p_rx[m, 0] + p_rx[m, 3])
        send(p_acc.at[m, 1 - zh], p_pair.at[m], pz_r.at[m], pair_x)

    def p_take(m):
        landed(p_pair.at[m], pz_r.at[m])
        p_own[pl.ds(pl.multiple_of(level_of(zl, m) * 32, 32), 32), :] = p_acc[m, zh] + p_pair[m]

    def y_tile(row):
        rows = pl.ds(pl.multiple_of(row, 384), 384)
        return mm(w[rows, :], vc[...].reshape(512, 768), 1, 1)

    def y_other(t):
        y_send[t] = y_tile((1 - k) * 768 + t * 384)
        send(y_send.at[t], y_core.at[t], yc_r.at[t], core)

    def y_mine(t):
        part = y_tile(k * 768 + t * 384)
        landed(y_core.at[t], yc_r.at[t])
        y_own[t] = (part + y_core[t]).reshape(4, 96, 512)
        ahead, behind = (1, 3) if t == 0 else (3, 1)
        send(y_own.at[t, (y + 2) % 4], y_far.at[t], yf_r.at[t], ring_y(ahead))
        send(y_own.at[t, (y + behind) % 4], y_rx.at[t, 1], y_r.at[t, 1], ring_y(behind))

    def y_hand_on(t):
        ahead = 1 if t == 0 else 3
        to = (y + ahead) % 4
        landed(y_far.at[t], yf_r.at[t])
        y_own[t, to] = y_own[t, to] + y_far[t]
        send(y_own.at[t, to], y_rx.at[t, 0], y_r.at[t, 0], ring_y(ahead))

    def y_sum(t):
        landed(y_rx.at[t, 0], y_r.at[t, 0])
        landed(y_rx.at[t, 1], y_r.at[t, 1])
        y_acc[t] = y_own[t, y] + (y_rx[t, 0] + y_rx[t, 1])

    p_tile(0)
    gather_vc.hand_on(1)
    gather_vr.take_far(1)
    gather_vr.take_core(1)
    p_tile(1)
    g_part[...] = mm(vr[0, c], vr[1].reshape(256, 1536), 1, 1)
    gather_vc.take_near(0)
    gather_vc.take_far(0)
    gather_vc.take_near(1)
    gather_vc.take_far(1)
    p_hand_on(0)

    def g_send(i, _):
        remote(g_part, g_rx.at[i], g_s.at[0], g_r.at[0], ((r + 1 + i) % 8, c)).start()
        return 0

    lax.fori_loop(0, 7, g_send, 0)
    y_other(0)
    y_other(1)
    p_hand_on(1)
    y_mine(0)
    p_sum(0)
    y_mine(1)
    y_hand_on(0)
    p_sum(1)

    landed(g_rx, g_r.at[0])
    g_own[...] = (g_part[...] + g_rx[0] + g_rx[1] + g_rx[2]) + (g_rx[3] + g_rx[4] + g_rx[5] + g_rx[6])
    g_all[c] = g_own[...]

    def g_spread(i, _):
        remote(g_own, g_all.at[c], g_s.at[1], g_r.at[1], (r, (c + 1 + i) % 16)).start()
        return 0

    lax.fori_loop(0, 15, g_spread, 0)
    y_hand_on(1)
    p_take(0)
    p_take(1)

    part = mm(p_own[...], vc[...].reshape(512, 768), 1, 1)
    s_part[0] = part[:, :256]
    s_part[1] = part[:, 256:]

    def chunk(ref, who):
        return ref.at[who % 2, pl.ds(pl.multiple_of(who // 2 * 8, 8), 8)]

    def s_send(i, _):
        to = (c + 1 + i) % 16
        remote(chunk(s_part, to), s_rx.at[i], g_s.at[2], g_r.at[2], (r, to)).start()
        return 0

    lax.fori_loop(0, 15, s_send, 0)
    y_sum(0)
    y_sum(1)
    send(y_acc.at[1 - zl], y_pair, yz_r.at[0], pair_y)

    landed(g_all.at[pl.ds(0, 15)], g_r.at[1])
    tc[0:256, 0:256] = tf[0]
    tc[256:512, 256:512] = tf[1]
    tc[256:512, 0:256] = jnp.zeros((256, 256), F32)
    tc[0:256, 256:512] = -mm(mm(tf[0], g_all[...].reshape(256, 256), 1, 0), tf[1], 1, 0)

    landed(s_rx, g_r.at[2])
    total = s_part[k, pl.ds(pl.multiple_of(c // 2 * 8, 8), 8)]
    for i in range(15):
        total = total + s_rx[i]
    s_own[...] = total
    s_all[k, pl.ds(pl.multiple_of(c // 2 * 8, 8), 8)] = total

    def s_spread(i, _):
        remote(s_own, chunk(s_all, c), g_s.at[3], g_r.at[3], (r, (c + 1 + i) % 16)).start()
        return 0

    lax.fori_loop(0, 15, s_spread, 0)

    landed(y_pair, yz_r.at[0])
    z_place = lambda l, d, o, q: z_all.at[z_index(l, d, o), pl.ds(q * 48, 48)]
    z_all[z_index(0, 0, 0)] = mm(y_acc[zl] + y_pair[...], tc[...], 1, 0)
    gather_z = Gather(lambda q: z_place(0, 0, 0, q), z_place, ring_y, pair_y, core, send, za_r)
    gather_z.start()

    landed(s_rx, g_r.at[3])
    s_rows = jnp.concatenate([s_all[0], s_all[1]], axis=1)
    mine = p_own[...] - mm(mm(s_rows, tc[...], 1, 0), vc[...].reshape(512, 768), 1, 0)

    def p_place(l, d, o, q):
        who = row_index(l, d)
        return p_all.at[who // 4, q, who % 4]

    for q in range(2):
        p_all[r // 4, q, r % 4] = mine[q * 32:(q + 1) * 32]
    gather_p = Gather(lambda q: p_place(0, 0, 0, q), p_place, ring_x, pair_x, None, send, pa_r)
    gather_p.start()

    def vv_tile(i):
        cols = slice(i * 512, (i + 1) * 512)
        vv[:, cols] = mm(tc[...], vr[...].reshape(512, 1536)[:, cols], 1, 0)

    def z_tile(level, other):
        first = level_of(k, other) * 8 + level_of(zl, level) * 4
        rows = pl.ds(pl.multiple_of(first * 96, 384), 384)
        w[rows, :] = w[rows, :] - mm(z_all[pl.ds(first, 4)].reshape(384, 512), vc[...].reshape(512, 768), 1, 0)

    gather_z.hand_on(0)
    gather_z.relay_pair()
    gather_p.hand_on(0)
    gather_p.relay_pair()
    vv_tile(0)
    gather_z.take_near(0)
    gather_z.hand_on(1)
    gather_z.take_far(0)
    gather_p.hand_on(1)
    gather_z.take_near(1)
    vv_tile(1)
    gather_z.take_far(1)
    vv_tile(2)
    z_tile(0, 0)
    z_tile(1, 0)
    gather_z.take_core(0)
    z_tile(0, 1)
    gather_z.take_core(1)
    z_tile(1, 1)
    gather_p.take_near(0)
    gather_p.take_far(0)
    gather_p.take_near(1)
    gather_p.take_far(1)

    for away, far in halves:
        pl.when(away)(far.wait_send)
    send.finish()
    landed(g_rx, g_s.at[0])
    landed(g_all.at[pl.ds(0, 15)], g_s.at[1])
    landed(s_rx, g_s.at[2])
    landed(s_rx, g_s.at[3])


def last(w, vv, p_all, out, done, sem):
    outs = []
    for i in range(4):
        rows = slice(i * 384, (i + 1) * 384)
        done[rows, :] = w[rows, :] - mm(vv[:, rows], p_all[...].reshape(512, 768), 0, 0)
        copy = pltpu.make_async_copy(done.at[pl.ds(i * 384, 384)], out.at[pl.ds(i * 384, 384)], sem.at[i])
        copy.start()
        outs.append(copy)
    for copy in outs:
        copy.wait()


def body(window, reflectors, factors):
    vt = jnp.swapaxes(reflectors, 1, 2)
    dma = pltpu.SemaphoreType.DMA
    vmem = lambda *s: pltpu.VMEM(s, F32)
    parts = pl.pallas_call(
        kernel,
        out_shape=[jax.ShapeDtypeStruct(q, F32) for q in ((1536, 768), (512, 1536), (2, 2, 4, 32, 768))],
        in_specs=[pl.BlockSpec(memory_space=pltpu.HBM)] * 3,
        out_specs=[pl.BlockSpec(memory_space=pltpu.VMEM)] * 3,
        scratch_shapes=[
            vmem(2, 16, 16, 1536), vmem(2, 16, 16, 768), vmem(2, 256, 256), vmem(512, 512),
            vmem(2, 4, 2, 32, 768), vmem(2, 2, 32, 768), vmem(2, 4, 32, 768), vmem(2, 2, 32, 768),
            vmem(2, 32, 768), vmem(64, 768),
            vmem(2, 384, 512), vmem(2, 384, 512), vmem(2, 4, 96, 512), vmem(2, 96, 512), vmem(2, 2, 96, 512),
            vmem(2, 96, 512), vmem(96, 512), vmem(16, 96, 512),
            vmem(16, 256), vmem(7, 16, 256), vmem(16, 256), vmem(16, 16, 256),
            vmem(2, 64, 256), vmem(15, 8, 256), vmem(8, 256), vmem(2, 64, 256),
            dma((3,)), dma((2,)), dma((2,)), dma((120,)), dma((32,)), dma((16,)), dma((16,)), dma((32,)),
            dma((2, 2)), dma((2, 4)), dma((2,)), dma((2,)), dma((2,)), dma((2, 2)), dma((1,)),
            dma((4,)), dma((4,)),
        ],
        compiler_params=pltpu.CompilerParams(
            has_side_effects=True, collective_id=0, vmem_limit_bytes=40 * 1024 * 1024
        ),
    )(window, vt, factors)
    return pl.pallas_call(
        last,
        out_shape=jax.ShapeDtypeStruct(window.shape, F32),
        in_specs=[pl.BlockSpec(memory_space=pltpu.VMEM)] * 3,
        out_specs=pl.BlockSpec(memory_space=pl.ANY),
        scratch_shapes=[pltpu.VMEM(window.shape, F32), dma((4,))],
        compiler_params=pltpu.CompilerParams(vmem_limit_bytes=14 * 1024 * 1024),
    )(*parts)


def solution(mesh):
    placed = (P("row", "col"), P(None, "row", "col"), P())
    return jax.shard_map(body, mesh=mesh, in_specs=placed, out_specs=P("row", "col"), check_vma=False)
```

time: 126 us -> 100 us (0.79)
  the two profiles are of different devices: /device:TPU:1 before, /device:TPU:16 now
where the time goes in v3:
time: 100 us
  Pallas kernels  98.2 us (98%)
  local copies, waits for them, and re-layouts  1.97 us (2%)
    pallas_call x1, Pallas kernels, body(): pl.pallas_call(kernel, out_shape=[jax.ShapeDtypeStruct(q, F32) for q in (...  92.8 us
    pallas_call x1, Pallas kernels, body(): pl.pallas_call(last, out_shape=jax.ShapeDtypeStruct(window.shape, F32), i...  5.35 us

profile of v3, /device:TPU:16, one launch (start us, length us, event | category | flops | bytes accessed | tf_op | source)
XLA Modules:
  0.0 100.3 jit_solution(10699616998777391940)
XLA Ops:
  0.0 0.0 copy-start
  0.0 1.0 %copy-done = f32[2,256,256]{2,1,0:T(8,128)S(1)} copy-done((f32[2,256,256]{2,1,0:T(8,128)S(1)}, f32[2,256,256]{2,1,0:T(8,128)}, u32[]{:S(2)}) %copy-start) | copy-done | bytes 524312
  1.0 0.0 copy-start.1
  1.0 0.9 copy-done.1
  2.0 92.8 %shard_map.37 = (f32[1536,768]{1,0:T(8,128)S(1)}, f32[512,1536]{1,0:T(8,128)S(1)}, f32[2,2,4,32,768]{4,3,2,1,0:T(8,128)S(1)}) custom-call(f32[1536,768]{1,0:T(8,128)} %w_hbm.1, f32[2,16,1536]{2,1,0:T(8,128)S(1)} %bitcast.1, f32[2,256,256]{2,1,0:T(8,128)S(1)} %copy-done), custom_call_target="tpu_custom_call" | custom-call | tf_op jit(solution)/shard_map/pallas_call | solution.py:407
  94.8 5.4 %shard_map.38 = f32[1536,768]{1,0:T(8,128)} custom-call(f32[1536,768]{1,0:T(8,128)S(1)} %get-tuple-element.8.w, f32[512,1536]{1,0:T(8,128)S(1)} %get-tuple-element.9.vv, f32[2,2,4,32,768]{4,3,2,1,0:T(8,128)S(1)} %get-tuple-element.10.p_all), custom_call_target="tpu_custom_call" | custom-call | tf_op jit(solution)/shard_map/pallas_call | solution.py:428
Async XLA Ops:
  0.0 1.0 %copy-start = (f32[2,256,256]{2,1,0:T(8,128)S(1)}, f32[2,256,256]{2,1,0:T(8,128)}, u32[]{:S(2)}) copy-start(f32[2,256,256]{2,1,0:T(8,128)} %t_hbm.1) | copy-start | bytes 1572868
  1.0 0.9 copy-start.1

commit v4 on v3

v4 whole, which is shorter than its diff:
```python
import jax
import jax.numpy as jnp
from jax import lax
from jax.experimental import pallas as pl
from jax.experimental.pallas import tpu as pltpu
from jax.sharding import PartitionSpec as P

MESH = pl.DeviceIdType.MESH
F32 = jnp.float32
HIGH = lax.Precision.HIGH


def mm(a, b, ca, cb):
    return lax.dot_general(a, b, (((ca,), (cb,)), ((), ())), precision=HIGH, preferred_element_type=F32)


def remote(src, dst, ssem, rsem, dev):
    return pltpu.make_async_remote_copy(
        src_ref=src, dst_ref=dst, send_sem=ssem, recv_sem=rsem, device_id=dev, device_id_type=MESH
    )


def landed(ref, sem):
    pltpu.make_async_copy(ref, ref, sem).wait()


class Sends:
    def __init__(self, ssem):
        self.ssem, self.started = ssem, []

    def __call__(self, src, dst, rsem, dev):
        copy = remote(src, dst, self.ssem.at[len(self.started)], rsem, dev)
        copy.start()
        self.started.append(copy)

    def finish(self):
        for copy in self.started:
            copy.wait_send()


class Gather:
    def __init__(self, own, place, ring, pair, core, send, rsem):
        self.own, self.place, self.ring, self.pair, self.core = own, place, ring, pair, core
        self.send, self.rsem = send, rsem

    def sem(self, level, d, q, other=0):
        return self.rsem.at[other * 16 + level * 8 + d * 2 + q]

    def start_first(self):
        place = self.place(0, 0, 0, 0)
        self.send(self.own(0), place, self.sem(1, 0, 0), self.pair)
        self.send(self.own(0), place, self.sem(0, 1, 0), self.ring(1))

    def start_second(self):
        place = self.place(0, 0, 0, 1)
        self.send(self.own(1), place, self.sem(1, 0, 1), self.pair)
        self.send(self.own(1), place, self.sem(0, 3, 1), self.ring(3))
        self.send(self.own(1), place, self.sem(0, 1, 1), self.ring(1))
        self.send(self.own(0), self.place(0, 0, 0, 0), self.sem(0, 3, 0), self.ring(3))
        if self.core is not None:
            for q in (0, 1):
                self.send(self.own(q), self.place(0, 0, 0, q), self.sem(0, 0, q, 1), self.core)

    def wait(self, level, d, q, other=0):
        landed(self.place(level, d, other, q), self.sem(level, d, q, other))

    def to_core(self, level, d, q):
        if self.core is not None:
            place = self.place(level, d, 0, q)
            self.send(place, place, self.sem(level, d, q, 1), self.core)

    def hand_on(self, level, q):
        d = 1 if q == 0 else 3
        self.wait(level, d, q)
        place = self.place(level, d, 0, q)
        self.send(place, place, self.sem(level, 2, q), self.ring(d))
        self.to_core(level, d, q)

    def relay_pair(self):
        first, second = self.place(1, 0, 0, 0), self.place(1, 0, 0, 1)
        self.wait(1, 0, 0)
        self.send(first, first, self.sem(1, 1, 0), self.ring(1))
        self.wait(1, 0, 1)
        self.send(second, second, self.sem(1, 3, 1), self.ring(3))
        self.send(second, second, self.sem(1, 1, 1), self.ring(1))
        self.send(first, first, self.sem(1, 3, 0), self.ring(3))
        self.to_core(1, 0, 0)
        self.to_core(1, 0, 1)

    def take_near(self, level, q):
        d = 3 if q == 0 else 1
        self.wait(level, d, q)
        self.to_core(level, d, q)

    def take_far(self, level, q):
        self.wait(level, 2, q)
        self.to_core(level, 2, q)

    def take_core(self, level, q):
        for d in (0, 1, 3, 2):
            self.wait(level, d, q, 1)


def kernel(
    w_hbm, v_hbm, t_hbm, w, vv, p_all,
    vr, vc, tf, tc,
    p, p_far, p_rx, p_acc, p_pair, p_own,
    y_send, y_core, y_own, y_far, y_rx, y_acc, y_pair, z_all,
    g_part, g_rx, g_own, g_all, s_part, s_rx, s_own, s_all,
    load_sem, zero_s, zero_r, all_s, vr_r, vc_r, pa_r, za_r,
    pf_r, p_r, pz_r, yc_r, yf_r, y_r, yz_r, g_s, g_r,
):
    r = lax.axis_index("row")
    c = lax.axis_index("col")
    x, zh = r // 2, r % 2
    zl, y, k = c // 8, (c // 2) % 4, c % 2

    def dev(x_, zh_, zl_, y_, k_):
        return (x_ * 2 + zh_, (zl_ * 4 + y_) * 2 + k_)

    def ring_x(d):
        return dev((x + d) % 4, zh, zl, y, k)

    def ring_y(d):
        return dev(x, zh, zl, (y + d) % 4, k)

    pair_x = dev(x, 1 - zh, zl, y, k)
    pair_y = dev(x, zh, 1 - zl, y, k)
    core = dev(x, zh, zl, y, 1 - k)

    def level_of(z, level):
        return z if level == 0 else 1 - z

    def col_index(level, d, other):
        return (level_of(zl, level) * 4 + (y + 4 - d) % 4) * 2 + level_of(k, other)

    def row_index(level, d):
        return ((x + 4 - d) % 4) * 2 + level_of(zh, level)

    def vc_pair(level, d):
        other_x = (x + 4 - d) % 4
        return (level_of(zh, level) + c // 2) % 2 * 4 + (other_x + 4 - c // 4) % 4

    load_w = pltpu.make_async_copy(w_hbm, w, load_sem.at[1])
    load_w.start()
    own_v = pltpu.make_async_copy(v_hbm, vr.at[:, c], load_sem.at[0])
    own_v.start()
    load_t = pltpu.make_async_copy(t_hbm, tf, load_sem.at[2])
    load_t.start()

    target = (x + y) % 4 * 2 + (zh + zl) % 2
    share = vc_pair(0, 0)
    barrier = pltpu.get_barrier_semaphore()

    def greet(device):
        pl.semaphore_signal(barrier, inc=1, device_id=device, device_id_type=MESH)

    for h in range(2):
        apart = jnp.logical_not(jnp.logical_and(target == r, 2 * r + h == c))
        pl.when(apart)(lambda h=h: greet((target, 2 * r + h)))
        apart = jnp.logical_not(jnp.logical_and(c // 2 == r, 2 * share + h == c))
        pl.when(apart)(lambda h=h: greet((c // 2, 2 * share + h)))
    for device in (ring_y(1), ring_y(3), pair_y, core):
        greet(device)
    for i in range(1, 8):
        greet(((r + i) % 8, c))
    home = jnp.logical_and(r == 0, c // 2 == 0)
    pl.semaphore_wait(barrier, 15 - 2 * home.astype(jnp.int32))

    halves = []
    for q in range(2):
        for h in range(2):
            src = v_hbm.at[q, :, pl.ds(h * 768, 768)]
            at_home = jnp.logical_and(target == r, 2 * r + h == c)
            away = jnp.logical_not(at_home)
            local = pltpu.make_async_copy(src, vc.at[q, c], zero_r.at[k, q])
            far = remote(src, vc.at[q, c], zero_s.at[h, q], zero_r.at[k, q], (target, 2 * r + h))
            pl.when(at_home)(local.start)
            pl.when(away)(far.start)
            halves.append((away, far))
    send = Sends(all_s)
    vr_place = lambda panel: lambda l, d, o, q: vr.at[panel, col_index(l, d, o), pl.ds(q * 8, 8)]
    vr0, vr1 = (
        Gather(
            lambda q, i=i: v_hbm.at[i, pl.ds(q * 8, 8)], vr_place(i), ring_y, pair_y, core, send, vr_r.at[i]
        )
        for i in range(2)
    )
    for gather in (vr0, vr1):
        gather.start_first()
        gather.start_second()

    def vc_gather(panel):
        place = lambda l, d, o, q: vc.at[panel, 2 * vc_pair(l, d) + q]
        return Gather(lambda q: place(0, 0, 0, q), place, ring_x, pair_x, None, send, vc_r.at[panel])

    vc0, vc1 = vc_gather(0), vc_gather(1)

    def vc_start(panel):
        gather = vc1 if panel else vc0
        for q in range(2):
            landed(vc.at[panel, 2 * share + q], zero_r.at[q, panel])
            (gather.start_second if q else gather.start_first)()

    def both(step, *where):
        for q in range(2):
            step(*where, q)

    vc_start(0)
    both(vr0.hand_on, 0)
    vr0.relay_pair()
    vc_start(1)
    both(vr1.hand_on, 0)
    vr1.relay_pair()
    both(vc0.hand_on, 0)
    both(vr0.take_near, 0)
    both(vr0.hand_on, 1)
    vc0.relay_pair()
    both(vr0.take_far, 0)
    both(vr1.take_near, 0)
    both(vc1.hand_on, 0)
    both(vr1.hand_on, 1)
    vc1.relay_pair()
    both(vr0.take_near, 1)
    both(vr0.take_far, 1)
    both(vr1.take_far, 0)
    own_v.wait()
    load_w.wait()
    load_t.wait()

    def p_product(m, n):
        cols = slice(n * 256, n * 256 + 256)
        p[m, :, :, :, cols] = mm(vr[m].reshape(256, 1536), w[:, cols], 1, 0).reshape(4, 2, 32, 256)

    def p_start(m):
        right, left, far = (x + 1) % 4, (x + 3) % 4, (x + 2) % 4
        send(p.at[m, far, 0], p_far.at[m, 0], pf_r.at[m, 0], ring_x(1))
        send(p.at[m, far, 1], p_far.at[m, 1], pf_r.at[m, 1], ring_x(3))
        send(p.at[m, right, 1], p_rx.at[m, 0], p_r.at[m, 0], ring_x(1))
        send(p.at[m, left, 0], p_rx.at[m, 1], p_r.at[m, 1], ring_x(3))

    def p_hand_on(m):
        right, left = (x + 1) % 4, (x + 3) % 4
        landed(p_far.at[m, 0], pf_r.at[m, 0])
        p[m, right, 0] = p[m, right, 0] + p_far[m, 0]
        send(p.at[m, right, 0], p_rx.at[m, 2], p_r.at[m, 2], ring_x(1))
        landed(p_far.at[m, 1], pf_r.at[m, 1])
        p[m, left, 1] = p[m, left, 1] + p_far[m, 1]
        send(p.at[m, left, 1], p_rx.at[m, 3], p_r.at[m, 3], ring_x(3))

    def p_sum(m):
        for i in range(4):
            landed(p_rx.at[m, i], p_r.at[m, i])
        p_acc[m, 0] = p[m, x, 0] + (p_rx[m, 1] + p_rx[m, 2])
        p_acc[m, 1] = p[m, x, 1] + (p_rx[m, 0] + p_rx[m, 3])
        send(p_acc.at[m, 1 - zh], p_pair.at[m], pz_r.at[m], pair_x)

    def p_take(m):
        landed(p_pair.at[m], pz_r.at[m])
        p_own[m * 32:(m + 1) * 32, :] = p_acc[m, zh] + p_pair[m]

    def y_tile(panel, row):
        rows = pl.ds(pl.multiple_of(row, 384), 384)
        return mm(w[rows, :], vc[panel].reshape(256, 768), 1, 1)

    def y_other(i, t):
        y_send[i, t] = y_tile(i, (1 - k) * 768 + t * 384)
        send(y_send.at[i, t], y_core.at[i, t], yc_r.at[i, t], core)

    def y_mine(i, t):
        part = y_tile(i, k * 768 + t * 384)
        landed(y_core.at[i, t], yc_r.at[i, t])
        y_own[i, t] = (part + y_core[i, t]).reshape(4, 2, 48, 256)
        send(y_own.at[i, t, (y + 2) % 4], y_far.at[i, t], yf_r.at[i, t], ring_y(3 if t else 1))

    def y_plain(i):
        for t, behind in ((1, 1), (0, 3)):
            send(y_own.at[i, t, (y + behind) % 4], y_rx.at[i, t, 1], y_r.at[i, t, 1], ring_y(behind))

    def y_hand_on(i, t):
        ahead = 1 if t == 0 else 3
        to = (y + ahead) % 4
        landed(y_far.at[i, t], yf_r.at[i, t])
        y_own[i, t, to] = y_own[i, t, to] + y_far[i, t]
        send(y_own.at[i, t, to], y_rx.at[i, t, 0], y_r.at[i, t, 0], ring_y(ahead))

    def y_sum(i, t):
        landed(y_rx.at[i, t, 0], y_r.at[i, t, 0])
        landed(y_rx.at[i, t, 1], y_r.at[i, t, 1])
        y_acc[i, t] = y_own[i, t, y] + (y_rx[i, t, 0] + y_rx[i, t, 1])
        send(y_acc.at[i, t, 1 - zl], y_pair.at[i, t], yz_r.at[i, t], pair_y)

    def vv_tile(i):
        cols = slice(i * 512, (i + 1) * 512)
        vv[:, cols] = mm(tc[...], vr[...].reshape(512, 1536)[:, cols], 1, 0)

    def g_product():
        g_part[...] = mm(vr[0, c], vr[1].reshape(256, 1536), 1, 1)

        def each(i, _):
            remote(g_part, g_rx.at[i], g_s.at[0], g_r.at[0], ((r + 1 + i) % 8, c)).start()
            return 0

        lax.fori_loop(0, 7, each, 0)

    def g_sum():
        landed(g_rx, g_r.at[0])
        g_own[...] = (g_part[...] + g_rx[0] + g_rx[1] + g_rx[2]) + (g_rx[3] + g_rx[4] + g_rx[5] + g_rx[6])
        g_all[c] = g_own[...]

        def each(i, _):
            remote(g_own, g_all.at[c], g_s.at[1], g_r.at[1], (r, (c + 1 + i) % 16)).start()
            return 0

        lax.fori_loop(0, 15, each, 0)

    def join_factors():
        landed(g_all.at[pl.ds(0, 15)], g_r.at[1])
        tc[0:256, 0:256] = tf[0]
        tc[256:512, 256:512] = tf[1]
        tc[256:512, 0:256] = jnp.zeros((256, 256), F32)
        tc[0:256, 256:512] = -mm(mm(tf[0], g_all[...].reshape(256, 256), 1, 0), tf[1], 1, 0)

    def chunk(ref, who):
        return ref.at[who % 2, pl.ds(pl.multiple_of(who // 2 * 8, 8), 8)]

    def s_product():
        part = mm(p_own[...], vc[...].reshape(512, 768), 1, 1)
        s_part[0] = part[:, :256]
        s_part[1] = part[:, 256:]

        def each(i, _):
            to = (c + 1 + i) % 16
            remote(chunk(s_part, to), s_rx.at[i], g_s.at[2], g_r.at[2], (r, to)).start()
            return 0

        lax.fori_loop(0, 15, each, 0)

    def s_sum():
        landed(s_rx, g_r.at[2])
        total = s_part[k, pl.ds(pl.multiple_of(c // 2 * 8, 8), 8)]
        for i in range(15):
            total = total + s_rx[i]
        s_own[...] = total
        s_all[k, pl.ds(pl.multiple_of(c // 2 * 8, 8), 8)] = total

        def each(i, _):
            remote(s_own, chunk(s_all, c), g_s.at[3], g_r.at[3], (r, (c + 1 + i) % 16)).start()
            return 0

        lax.fori_loop(0, 15, each, 0)

    def z_place(level, d, other, q):
        return z_all.at[level_of(k, other), q, (y + 4 - d) % 4, level_of(zl, level)]

    gather_z = Gather(lambda q: z_place(0, 0, 0, q), z_place, ring_y, pair_y, core, send, za_r)

    def z_start(t):
        for i in range(2):
            landed(y_pair.at[i, t], yz_r.at[i, t])
        rows = jnp.concatenate([y_acc[i, t, zl] + y_pair[i, t] for i in range(2)], axis=1)
        z_all[k, t, y, zl] = mm(rows, tc[...], 1, 0)
        (gather_z.start_second if t else gather_z.start_first)()

    def z_tile(other, t):
        half = level_of(k, other)
        rows = pl.ds(pl.multiple_of(half * 768 + t * 384, 384), 384)
        w[rows, :] = w[rows, :] - mm(z_all[half, t].reshape(384, 512), vc[...].reshape(512, 768), 1, 0)

    def p_place(level, d, other, q):
        return p_all.at[q, row_index(level, d)]

    gather_p = Gather(lambda q: p_place(0, 0, 0, q), p_place, ring_x, pair_x, None, send, pa_r)

    def p_correct():
        landed(s_rx, g_r.at[3])
        s_rows = jnp.concatenate([s_all[0], s_all[1]], axis=1)
        mine = p_own[...] - mm(mm(s_rows, tc[...], 1, 0), vc[...].reshape(512, 768), 1, 0)
        for q in range(2):
            p_all[q, r] = mine[q * 32:(q + 1) * 32]
        gather_p.start_first()
        gather_p.start_second()

    both(vr0.take_core, 0)
    both(vr0.take_core, 1)
    p_product(0, 0)
    both(vr1.take_near, 1)
    both(vr1.take_far, 1)
    both(vc0.hand_on, 1)
    p_product(0, 1)
    p_product(0, 2)
    p_start(0)
    both(vc1.hand_on, 1)
    for level in range(2):
        both(vc0.take_near, level)
        both(vc0.take_far, level)
    y_other(0, 0)
    y_other(0, 1)
    both(vr1.take_core, 0)
    both(vr1.take_core, 1)
    g_product()
    for n in range(3):
        p_product(1, n)
    p_start(1)
    y_mine(0, 0)
    y_mine(0, 1)
    y_plain(0)
    p_hand_on(0)
    g_sum()
    for level in range(2):
        both(vc1.take_near, level)
        both(vc1.take_far, level)
    y_other(1, 0)
    y_other(1, 1)
    p_hand_on(1)
    y_hand_on(0, 0)
    y_hand_on(0, 1)
    y_mine(1, 0)
    y_mine(1, 1)
    y_plain(1)
    p_sum(0)
    join_factors()
    p_sum(1)
    y_hand_on(1, 0)
    y_hand_on(1, 1)
    y_sum(0, 0)
    y_sum(0, 1)
    p_take(0)
    p_take(1)
    s_product()
    y_sum(1, 0)
    y_sum(1, 1)
    s_sum()
    z_start(0)
    z_start(1)
    p_correct()
    both(gather_z.hand_on, 0)
    gather_z.relay_pair()
    vv_tile(0)
    both(gather_p.hand_on, 0)
    gather_p.relay_pair()
    vv_tile(1)
    both(gather_z.take_near, 0)
    both(gather_z.hand_on, 1)
    vv_tile(2)
    both(gather_z.take_far, 0)
    both(gather_p.hand_on, 1)
    both(gather_z.take_near, 1)
    both(gather_z.take_far, 1)
    z_tile(0, 0)
    z_tile(0, 1)
    for q in range(2):
        for level in range(2):
            gather_z.take_core(level, q)
        z_tile(1, q)
    for level in range(2):
        both(gather_p.take_near, level)
        both(gather_p.take_far, level)

    for away, far in halves:
        pl.when(away)(far.wait_send)
    send.finish()
    landed(g_rx, g_s.at[0])
    landed(g_all.at[pl.ds(0, 15)], g_s.at[1])
    landed(s_rx, g_s.at[2])
    landed(s_rx, g_s.at[3])


def last(w, vv, p_all, out, done, sem):
    outs = []
    for i in range(4):
        rows = slice(i * 384, (i + 1) * 384)
        done[rows, :] = w[rows, :] - mm(vv[:, rows], p_all[...].reshape(512, 768), 0, 0)
        copy = pltpu.make_async_copy(done.at[pl.ds(i * 384, 384)], out.at[pl.ds(i * 384, 384)], sem.at[i])
        copy.start()
        outs.append(copy)
    for copy in outs:
        copy.wait()


def body(window, reflectors, factors):
    vt = jnp.swapaxes(reflectors, 1, 2)
    dma = pltpu.SemaphoreType.DMA
    vmem = lambda *s: pltpu.VMEM(s, F32)
    parts = pl.pallas_call(
        kernel,
        out_shape=[jax.ShapeDtypeStruct(q, F32) for q in ((1536, 768), (512, 1536), (2, 8, 32, 768))],
        in_specs=[pl.BlockSpec(memory_space=pltpu.HBM)] * 3,
        out_specs=[pl.BlockSpec(memory_space=pltpu.VMEM)] * 3,
        scratch_shapes=[
            vmem(2, 16, 16, 1536), vmem(2, 16, 16, 768), vmem(2, 256, 256), vmem(512, 512),
            vmem(2, 4, 2, 32, 768), vmem(2, 2, 32, 768), vmem(2, 4, 32, 768), vmem(2, 2, 32, 768),
            vmem(2, 32, 768), vmem(64, 768),
            vmem(2, 2, 384, 256), vmem(2, 2, 384, 256), vmem(2, 2, 4, 2, 48, 256), vmem(2, 2, 2, 48, 256),
            vmem(2, 2, 2, 2, 48, 256), vmem(2, 2, 2, 48, 256), vmem(2, 2, 48, 256), vmem(2, 2, 4, 2, 48, 512),
            vmem(16, 256), vmem(7, 16, 256), vmem(16, 256), vmem(16, 16, 256),
            vmem(2, 64, 256), vmem(15, 8, 256), vmem(8, 256), vmem(2, 64, 256),
            dma((3,)), dma((2, 2)), dma((2, 2)), dma((180,)), dma((2, 32)), dma((2, 16)), dma((16,)), dma((32,)),
            dma((2, 2)), dma((2, 4)), dma((2,)), dma((2, 2)), dma((2, 2)), dma((2, 2, 2)), dma((2, 2)),
            dma((4,)), dma((4,)),
        ],
        compiler_params=pltpu.CompilerParams(
            has_side_effects=True, collective_id=0, vmem_limit_bytes=40 * 1024 * 1024
        ),
    )(*(pltpu.with_memory_space_constraint(a, pltpu.HBM) for a in (window, vt, factors)))
    return pl.pallas_call(
        last,
        out_shape=jax.ShapeDtypeStruct(window.shape, F32),
        in_specs=[pl.BlockSpec(memory_space=pltpu.VMEM)] * 3,
        out_specs=pl.BlockSpec(memory_space=pl.ANY),
        scratch_shapes=[pltpu.VMEM(window.shape, F32), dma((4,))],
        compiler_params=pltpu.CompilerParams(vmem_limit_bytes=14 * 1024 * 1024),
    )(*parts)


def solution(mesh):
    placed = (P("row", "col"), P(None, "row", "col"), P())
    return jax.shard_map(body, mesh=mesh, in_specs=placed, out_specs=P("row", "col"), check_vma=False)
```

time: 100 us -> 94.4 us (0.944)
  the two profiles are of different devices: /device:TPU:16 before, /device:TPU:1 now
where the time goes in v4:
time: 94.4 us; the launch traced here: 94.2 us
  Pallas kernels  94 us (100%)
    pallas_call x1, Pallas kernels, body(): pl.pallas_call(kernel, out_shape=[jax.ShapeDtypeStruct(q, F32) for q in (...  88.7 us
    pallas_call x1, Pallas kernels, body(): pl.pallas_call(last, out_shape=jax.ShapeDtypeStruct(window.shape, F32), i...  5.35 us

profile of v4, /device:TPU:1, one launch (start us, length us, event | category | flops | bytes accessed | tf_op | source)
XLA Modules:
  0.0 94.2 jit_solution(1608543252012662023)
XLA Ops:
  0.0 88.7 %shard_map.37 = (f32[1536,768]{1,0:T(8,128)S(1)}, f32[512,1536]{1,0:T(8,128)S(1)}, f32[2,8,32,768]{3,2,1,0:T(8,128)S(1)}) custom-call(f32[1536,768]{1,0:T(8,128)} %w_hbm.1, f32[2,16,1536]{2,1,0:T(8,128)} %bitcast.1, f32[2,256,256]{2,1,0:T(8,128)} %t_hbm.1), custom_call_target="tpu_custom_call" | custom-call | tf_op jit(solution)/shard_map/pallas_call | solution.py:485
  88.7 5.4 %shard_map.38 = f32[1536,768]{1,0:T(8,128)} custom-call(f32[1536,768]{1,0:T(8,128)S(1)} %get-tuple-element.8.w, f32[512,1536]{1,0:T(8,128)S(1)} %get-tuple-element.9.vv, f32[2,8,32,768]{3,2,1,0:T(8,128)S(1)} %get-tuple-element.10.p_all), custom_call_target="tpu_custom_call" | custom-call | tf_op jit(solution)/shard_map/pallas_call | solution.py:506

commit v5 on v4

--- a/solution.py
+++ b/solution.py
@@ -468,10 +468,10 @@
 
 def last(w, vv, p_all, out, done, sem):
     outs = []
-    for i in range(4):
-        rows = slice(i * 384, (i + 1) * 384)
+    for i in range(6):
+        rows = slice(i * 256, (i + 1) * 256)
         done[rows, :] = w[rows, :] - mm(vv[:, rows], p_all[...].reshape(512, 768), 0, 0)
-        copy = pltpu.make_async_copy(done.at[pl.ds(i * 384, 384)], out.at[pl.ds(i * 384, 384)], sem.at[i])
+        copy = pltpu.make_async_copy(done.at[pl.ds(i * 256, 256)], out.at[pl.ds(i * 256, 256)], sem.at[i])
         copy.start()
         outs.append(copy)
     for copy in outs:
@@ -508,7 +508,7 @@
         out_shape=jax.ShapeDtypeStruct(window.shape, F32),
         in_specs=[pl.BlockSpec(memory_space=pltpu.VMEM)] * 3,
         out_specs=pl.BlockSpec(memory_space=pl.ANY),
-        scratch_shapes=[pltpu.VMEM(window.shape, F32), dma((4,))],
+        scratch_shapes=[pltpu.VMEM(window.shape, F32), dma((6,))],
         compiler_params=pltpu.CompilerParams(vmem_limit_bytes=14 * 1024 * 1024),
     )(*parts)
 

time: 94.4 us -> 94.3 us (level)
  no operation moved by 1% of the time
where the time goes in v5:
time: 94.3 us; the launch traced here: 94.2 us
  Pallas kernels  94 us (100%)
    pallas_call x1, Pallas kernels, body(): pl.pallas_call(kernel, out_shape=[jax.ShapeDtypeStruct(q, F32) for q in (...  88.7 us
    pallas_call x1, Pallas kernels, body(): pl.pallas_call(last, out_shape=jax.ShapeDtypeStruct(window.shape, F32), i...  5.28 us

profile of v5, /device:TPU:1, one launch (start us, length us, event | category | flops | bytes accessed | tf_op | source)
XLA Modules:
  0.0 94.2 jit_solution(7029037017964547085)
XLA Ops:
  0.0 88.7 %shard_map.37 = (f32[1536,768]{1,0:T(8,128)S(1)}, f32[512,1536]{1,0:T(8,128)S(1)}, f32[2,8,32,768]{3,2,1,0:T(8,128)S(1)}) custom-call(f32[1536,768]{1,0:T(8,128)} %w_hbm.1, f32[2,16,1536]{2,1,0:T(8,128)} %bitcast.1, f32[2,256,256]{2,1,0:T(8,128)} %t_hbm.1), custom_call_target="tpu_custom_call" | custom-call | tf_op jit(solution)/shard_map/pallas_call | solution.py:485
  88.7 5.3 %shard_map.38 = f32[1536,768]{1,0:T(8,128)} custom-call(f32[1536,768]{1,0:T(8,128)S(1)} %get-tuple-element.8.w, f32[512,1536]{1,0:T(8,128)S(1)} %get-tuple-element.9.vv, f32[2,8,32,768]{3,2,1,0:T(8,128)S(1)} %get-tuple-element.10.p_all), custom_call_target="tpu_custom_call" | custom-call | tf_op jit(solution)/shard_map/pallas_call | solution.py:506
